TPU v7x, 512 devices: a whole 4x4x16 slice. The times are simulated.
512 devices in a mesh: img: 16 (over x, z_hi), band: 32 (over y, z_lo, core).
Axes of the slice: x: 4, y: 4, z: 16 (z_hi: 4, z_lo: 4; z = z_hi * 4 + z_lo), core: 2. Of those that a mesh axis runs over, the one named last changes fastest.
Arguments:
- latents: bfloat16 [16, 64, 64, 1120], P('img', 'band'), may hold values from -6 to 6
- tangents: bfloat16 [16, 64, 64, 1120], P('img', 'band'), may hold values from -6 to 6
- w_expand: bfloat16 [1120, 5632], P('img', 'band'), may hold values from -0.1875 to 0.1875
- b_expand: bfloat16 [5632], P('band'), may hold values from -3 to 3
- w_depth: bfloat16 [9, 5632], P(None, 'band'), may hold values from -2 to 2
- b_depth: bfloat16 [5632], P('band'), may hold values from -3 to 3
Outputs:
- gated: bfloat16 [16, 64, 64, 2816], P('img', 'band')
- gated_tangent: bfloat16 [16, 64, 64, 2816], P('img', 'band')
All inputs are finite; a program needn't handle non-finite values.
Results may differ from a plain program's by a relative error of at most 0.0057.
Values may be sent and summed in bfloat16 or wider, within the bound.
No kernel may reach another device: no remote copies, remote signals or barrier semaphores. Data moves between devices by JAX's collectives and lax.ppermute only.
A program may use at most 64 MiB of HBM per device.

v0:
```python
import jax
import jax.numpy as jnp
from jax import lax
from jax.sharding import PartitionSpec as P


def extended(cells, sides, width):
    for axis, dim in sides:
        count = lax.axis_size(axis)
        ends = count - 1
        head = lax.slice_in_dim(cells, 0, width, axis=dim)
        tail = lax.slice_in_dim(cells, cells.shape[dim] - width, cells.shape[dim], axis=dim)
        cells = jnp.concatenate(
            [
                lax.ppermute(tail, axis, [(i, (i + 1) % count) for i in range(ends)]),
                cells,
                lax.ppermute(head, axis, [((i + 1) % count, i) for i in range(ends)]),
            ],
            axis=dim,
        )
    return cells


def tangent_act(primal_pre, tangent_pre):
    sigmoid_v = jax.nn.sigmoid(primal_pre)
    value = primal_pre * sigmoid_v
    slope = sigmoid_v * (1.0 + primal_pre * (1.0 - sigmoid_v))
    return (value, slope * tangent_pre)


def depthwise(padded, depth_taps, row_count, col_count):
    total = jnp.zeros(padded.shape[:-3] + (row_count, col_count, padded.shape[-1]), jnp.float32)
    for row_off in range(3):
        for col_off in range(3):
            window = padded[
                ..., row_off : row_off + row_count, col_off : col_off + col_count, :
            ].astype(jnp.float32)
            total = total + window * depth_taps[3 * row_off + col_off].astype(jnp.float32)
    return total


def finish(mixed, depth_bias, half):
    primal_mix = mixed[0] + depth_bias.astype(jnp.float32)
    tangent_mix = mixed[1]
    gate_value, gate_tangent = tangent_act(primal_mix[..., half:], tangent_mix[..., half:])
    gated = primal_mix[..., :half] * gate_value
    gated_tangent = tangent_mix[..., :half] * gate_value + primal_mix[..., :half] * gate_tangent
    return (gated.astype(jnp.bfloat16), gated_tangent.astype(jnp.bfloat16))


def activate(pre_act, expand_bias, token_count):
    bias_cols = expand_bias.astype(jnp.float32)
    value, slope_tangent = tangent_act(pre_act[:token_count] + bias_cols, pre_act[token_count:])
    return jnp.concatenate([value.astype(jnp.bfloat16), slope_tangent.astype(jnp.bfloat16)], 0)


def on_device(latents, tangents, w_expand, b_expand, w_depth, b_depth):
    image_count, row_count, col_count, channels = latents.shape
    depth_taps, expand_bias, depth_bias = (
        lax.all_gather(w_depth, "band", axis=1, tiled=True),
        lax.all_gather(b_expand, "band", axis=0, tiled=True),
        lax.all_gather(b_depth, "band", axis=0, tiled=True),
    )
    full_width = expand_bias.shape[0]
    half = full_width // 2
    both_inputs = jnp.stack([latents, tangents])
    span_rows = both_inputs.shape[2]
    token_count = image_count * span_rows * col_count
    stacked = both_inputs.reshape(2 * token_count, channels)
    weight_rows = lax.all_gather(w_expand, "img", axis=0, tiled=True)
    pre_act = jnp.dot(
        stacked,
        lax.all_gather(weight_rows, "band", axis=1, tiled=True),
        preferred_element_type=jnp.float32,
    )
    activated = activate(pre_act, expand_bias, token_count)
    activated = activated.reshape(2, image_count, span_rows, col_count, full_width)
    padded = extended(activated, (("band", 2),), 1)
    padded = jnp.pad(padded, ((0, 0), (0, 0), (0, 0), (1, 1), (0, 0)))
    mixed = depthwise(padded, depth_taps, row_count, col_count)
    return finish(mixed, depth_bias, half)


def solution(mesh):
    placed = (
        P("img", "band", None, None),
        P("img", "band", None, None),
        P("img", "band"),
        P("band"),
        P(None, "band"),
        P("band"),
    )
    return jax.shard_map(
        on_device,
        mesh=mesh,
        in_specs=placed,
        out_specs=(P("img", "band", None, None), P("img", "band", None, None)),
        check_vma=False,
    )
```

profile of v0, /device:TPU:33, one launch (start us, length us, event | category | flops | bytes accessed | tf_op | source)
XLA Modules:
  0.0 304.1 jit_solution(5817018077975962852)
XLA Ops:
  7.2 0.0 all-gather.4.cloned.1.call-start
  7.3 57.8 %all-gather = bf16[16,70,176]{2,1,0:T(8,128)(2,1)S(1)} all-gather(bf16[1,70,176]{2,1,0:T(8,128)(2,1)} %bitcast.34), channel_id=1, replica_groups=mesh['img'=16,'band'=32] {'img'}, dimensions={0}, use_global_device_ids=true | all-gather | bytes 418880 | tf_op jit(solution)/shard_map/all_gather | solution.py:70
  65.1 0.2 reshape.144
  65.3 1.0 copy.30
  66.3 0.0 all-gather.4.cloned.1.call-update
  66.3 1.3 dynamic-slice
  68.2 0.2 dynamic-update-slice
  68.5 0.0 copy-done.4
  68.5 0.2 dynamic-update-slice.1
  68.7 134.4 %all-reduce.3 = (bf16[5632]{0:T(1024)(128)(2,1)S(1)}, bf16[5632]{0:T(1024)(128)(2,1)S(1)}) all-reduce(bf16[5632]{0:T(1024)(128)(2,1)S(1)} %dynamic-update-slice, bf16[5632]{0:T(1024)(128)(2,1)S(1)} %dynamic-update-slice.1), channel_id=1, replica_groups=mesh['img'=16,'band'=32] {'band'}, use_global_device_ids=true, to_apply=%add.1 | all-reduce | flops 11264 | bytes 45056
  203.2 0.0 copy-done
  203.2 0.1 pad_maximum_fusion.3
  203.3 0.0 all-gather.4.cloned.1.call-done
  203.3 7.0 %fusion.22 = f32[256,5632]{1,0:T(8,128)S(1)} fusion(bf16[256,1120]{1,0:T(8,128)(2,1)S(1)} %bitcast.31, bf16[1120,5632]{0,1:T(8,128)(2,1)} %all-gather.4.cloned.1.call-done), kind=kOutput, calls=%fused_computation.48 | convolution fusion | flops 3229614080 | bytes 18956288 | tf_op jit(solution)/shard_map/dot_general | solution.py:71
  210.4 1.4 multiply_convert_fusion
  211.7 0.2 pad_maximum_fusion.2
  211.9 0.0 copy-start.2
  211.9 1.8 fusion.21
  213.7 8.1 %collective-permute-start.1 = (bf16[2,1,1,64,5632]{4,3,2,1,0:T(8,128)(2,1)}, bf16[2,1,1,64,5632]{4,3,2,1,0:T(8,128)(2,1)}, u32[]{:S(2)}, u32[]{:S(2)}) collective-permute-start(bf16[2,1,1,64,5632]{4,3,2,1,0:T(8,128)(2,1)} %get-tuple-element.18), channel_id=1, source_target_pairs={{1,0},{2,1},{3,2},{4,3},{5,4},{6,5},{7,6},{8,7},{9,8},{10,9},{11,1... | collective-permute-start | bytes 4325384 | tf_op jit(solution)/shard_map/ppermute | solution.py:17
  221.8 1.9 collective-permute-start
  223.7 0.0 copy-done.2
  223.7 59.7 %all-gather.1 = bf16[32,176,9]{1,2,0:T(8,128)(2,1)S(1)} all-gather(bf16[1,176,9]{1,2,0:T(8,128)(2,1)S(1)} %bitcast.35), channel_id=1, replica_groups=mesh['img'=16,'band'=32] {'band'}, dimensions={0}, use_global_device_ids=true | all-gather | bytes 104544 | tf_op jit(solution)/shard_map/all_gather | solution.py:60
  283.4 0.1 copy.26
  283.4 0.3 reshape.139
  283.7 0.6 fusion.20
  284.3 0.0 collective-permute-done.1
  284.3 0.0 collective-permute-done
  284.3 3.8 %fusion.5 = bf16[2,1,4,66,5632]{4,3,2,1,0:T(8,128)(2,1)S(1)} fusion(bf16[2,1,1,64,5632]{4,3,2,1,0:T(8,128)(2,1)} %collective-permute-done.1, bf16[2,1,2,64,5632]{4,3,2,1,0:T(8,128)(2,1)S(1)} %bitcast.28, bf16[2,1,1,64,5632]{4,3,2,1,0:T(8,128)(2,1)} %collective-permute-done), kind=kLoop, calls=%fused_computation.7 | loop fusion | flops 35684352 | bytes 11714560 | tf_op jit(solution)/shard_map/concatenate | solution.py:13
  288.2 6.8 %multiply_add_fusion = f32[2,1,2,64,5632]{4,3,2,1,0:T(8,128)S(1)} fusion(bf16[2,1,2,64,5632]{4,3,2,1,0:T(8,128)(2,1)S(1)} %bitcast.29, bf16[2,1,4,66,5632]{4,3,2,1,0:T(8,128)(2,1)S(1)} %fusion.5, bf16[2,1,1,64,5632]{4,3,2,1,0:T(8,128)(2,1)} %collective-permute-done.1, bf16[2,1,1,64,5632]{4,3,2,1,0:T(8,128)(2,1)} %collective-permute-done, ...), kind=kLoop, calls=%fused_computation.8 | loop fusion | flops 40370176 | bytes 29038592 | tf_op jit(solution)/shard_map/add | solution.py:38
  294.9 0.2 slice_bitcast_fusion
  295.1 0.3 fusion.6
  295.4 1.8 fusion.10
  (10 shorter events, 0.0 us)
Async XLA Ops:
  7.2 61.1 %copy-start.3 = (bf16[176]{0:T(256)(128)(2,1)S(1)}, bf16[176]{0:T(256)(128)(2,1)}, u32[]{:S(2)}) copy-start(bf16[176]{0:T(256)(128)(2,1)} %param.9) | copy-start | bytes 1060
  7.2 61.3 %copy-start.4 = (bf16[176]{0:T(256)(128)(2,1)S(1)}, bf16[176]{0:T(256)(128)(2,1)}, u32[]{:S(2)}) copy-start(bf16[176]{0:T(256)(128)(2,1)} %param.11) | copy-start | bytes 1060
  7.2 196.0 %copy-start = (bf16[1,2,64,1120]{3,2,1,0:T(8,128)(2,1)S(1)}, bf16[1,2,64,1120]{3,2,1,0:T(8,128)(2,1)}, u32[]{:S(2)}) copy-start(bf16[1,2,64,1120]{3,2,1,0:T(8,128)(2,1)} %param.7) | copy-start | bytes 860164
  7.2 196.0 %copy-start.1 = (bf16[1,2,64,1120]{3,2,1,0:T(8,128)(2,1)S(1)}, bf16[1,2,64,1120]{3,2,1,0:T(8,128)(2,1)}, u32[]{:S(2)}) copy-start(bf16[1,2,64,1120]{3,2,1,0:T(8,128)(2,1)} %param.6) | copy-start | bytes 860164
  7.2 196.1 %all-gather.4.cloned.1.call-start = ((), (), s32[]{:S(2)}) async-start(), calls=%async_computation | async-start | bytes 13381632 | tf_op jit(solution)/shard_map/all_gather | solution.py:73
  211.9 11.8 %copy-start.2 = (bf16[9,176]{1,0:T(8,128)(2,1)S(1)}, bf16[9,176]{1,0:T(8,128)(2,1)}, u32[]{:S(2)}) copy-start(bf16[9,176]{1,0:T(8,128)(2,1)} %param.10) | copy-start | bytes 9508
  213.7 70.6 %collective-permute-start.1 = (bf16[2,1,1,64,5632]{4,3,2,1,0:T(8,128)(2,1)}, bf16[2,1,1,64,5632]{4,3,2,1,0:T(8,128)(2,1)}, u32[]{:S(2)}, u32[]{:S(2)}) collective-permute-start(bf16[2,1,1,64,5632]{4,3,2,1,0:T(8,128)(2,1)} %get-tuple-element.18), channel_id=1, source_target_pairs={{1,0},{2,1},{3,2},{4,3},{5,4},{6,5},{7,6},{8,7},{9,8},{10,9},{11,1... | collective-permute-start | bytes 4325384 | tf_op jit(solution)/shard_map/ppermute | solution.py:17
  221.8 62.5 %collective-permute-start = (bf16[2,1,1,64,5632]{4,3,2,1,0:T(8,128)(2,1)}, bf16[2,1,1,64,5632]{4,3,2,1,0:T(8,128)(2,1)}, u32[]{:S(2)}, u32[]{:S(2)}) collective-permute-start(bf16[2,1,1,64,5632]{4,3,2,1,0:T(8,128)(2,1)} %get-tuple-element.17), channel_id=1, source_target_pairs={{0,1},{1,2},{2,3},{3,4},{4,5},{5,6},{6,7},{7,8},{8,9},{9,10},{10,1... | collective-permute-start | bytes 4325384 | tf_op jit(solution)/shard_map/ppermute | solution.py:15
Sparse Core Ops, SparseCore 0:
  66.4 89.6 all-gather.3
where the time goes:
time: 304 us
  blocking collectives  252 us (83%)
  other arithmetic  14.9 us (5%)
  between operations  14.9 us (5%)
  starting transfers between devices  10 us (3%)
  matrix products  7.05 us (2%)
  local copies, waits for them, and re-layouts  5.29 us (2%)
    unnamed x1, blocking collectives  134 us
    all_gather x1, blocking collectives, on_device(): lax.all_gather(w_depth, 'band', axis=1, tiled=True)  59.7 us
    all_gather x1, blocking collectives, on_device(): weight_rows = lax.all_gather(w_expand, 'img', axis=0, tiled=True)  57.8 us
    ppermute x1, starting transfers between devices, extended(): lax.ppermute(head, axis, [((i + 1) % count, i) for i in range(ends)])  8.08 us
    dot_general x1, matrix products, on_device(): jnp.dot(stacked, lax.all_gather(weight_rows, 'band', axis=1, tiled=True),...  7.05 us
    add x1, other arithmetic, depthwise(): total + window * depth_taps[3 * row_off + col_off].astype(jnp.float32)  6.78 us
  transfers between devices with their start and end apart: 3, of which 0 were waited for; matrix products, arithmetic and copies ran while one was open for 1% of the time, Pallas kernels for 0%

commit v1 on v0

--- a/solution.py
+++ b/solution.py
@@ -2,6 +2,11 @@
 import jax.numpy as jnp
 from jax import lax
 from jax.sharding import PartitionSpec as P
+
+
+def swapped_in(x, axis, dim):
+    sent = jnp.stack([x] * lax.axis_size(axis))
+    return jnp.concatenate(lax.all_to_all(sent, axis, 0, 0), axis=dim)
 
 
 def extended(cells, sides, width):
@@ -57,7 +62,7 @@
 def on_device(latents, tangents, w_expand, b_expand, w_depth, b_depth):
     image_count, row_count, col_count, channels = latents.shape
     depth_taps, expand_bias, depth_bias = (
-        lax.all_gather(w_depth, "band", axis=1, tiled=True),
+        swapped_in(w_depth, "band", 1),
         lax.all_gather(b_expand, "band", axis=0, tiled=True),
         lax.all_gather(b_depth, "band", axis=0, tiled=True),
     )

time: 304 us -> 277 us (0.911)
  the two profiles are of different devices: /device:TPU:33 before, /device:TPU:1 now
where the time goes in v1:
time: 277 us
  blocking collectives  199 us (72%)
  waiting for transfers between devices  17.8 us (6%)
  starting transfers between devices  15.3 us (6%)
  other arithmetic  15.2 us (5%)
  between operations  14.9 us (5%)
  local copies, waits for them, and re-layouts  7.26 us (3%)
  matrix products  7.05 us (3%)
    unnamed x1, blocking collectives  140 us
    all_gather x1, blocking collectives, on_device(): weight_rows = lax.all_gather(w_expand, 'img', axis=0, tiled=True)  59.5 us
    all_to_all x1, waiting for transfers between devices, swapped_in(): return jnp.concatenate(lax.all_to_all(sent, axis, 0, 0), axis=dim)  17.8 us
    ppermute x1, starting transfers between devices, extended(): lax.ppermute(head, axis, [((i + 1) % count, i) for i in range(ends)])  8.18 us
    dot_general x1, matrix products, on_device(): jnp.dot(stacked, lax.all_gather(weight_rows, 'band', axis=1, tiled=True),...  7.05 us
    add x1, other arithmetic, depthwise(): total + window * depth_taps[3 * row_off + col_off].astype(jnp.float32)  6.78 us
  transfers between devices with their start and end apart: 4, of which 1 were waited for; matrix products, arithmetic and copies ran while one was open for 2% of the time, Pallas kernels for 0%

profile of v1, /device:TPU:1, one launch (start us, length us, event | category | flops | bytes accessed | tf_op | source)
XLA Modules:
  0.0 276.6 jit_solution(14233562190022145726)
XLA Ops:
  7.3 59.5 %all-gather = bf16[16,70,176]{2,1,0:T(8,128)(2,1)S(1)} all-gather(bf16[1,70,176]{2,1,0:T(8,128)(2,1)} %bitcast.29), channel_id=1, replica_groups=mesh['img'=16,'band'=32] {'img'}, dimensions={0}, use_global_device_ids=true | all-gather | bytes 418880 | tf_op jit(solution)/shard_map/all_gather | solution.py:75
  66.7 0.2 reshape.167
  67.0 1.0 copy.28
  68.0 1.3 dynamic-slice
  69.9 0.2 dynamic-update-slice
  70.2 0.2 dynamic-update-slice.1
  70.4 139.7 %all-reduce.3 = (bf16[5632]{0:T(1024)(128)(2,1)S(1)}, bf16[5632]{0:T(1024)(128)(2,1)S(1)}) all-reduce(bf16[5632]{0:T(1024)(128)(2,1)S(1)} %dynamic-update-slice, bf16[5632]{0:T(1024)(128)(2,1)S(1)} %dynamic-update-slice.1), channel_id=1, replica_groups=mesh['img'=16,'band'=32] {'band'}, use_global_device_ids=true, to_apply=%add.1 | all-reduce | flops 11264 | bytes 45056
  210.2 7.0 %fusion.22 = f32[256,5632]{1,0:T(8,128)S(1)} fusion(bf16[256,1120]{1,0:T(8,128)(2,1)S(1)} %bitcast.26, bf16[1120,5632]{0,1:T(8,128)(2,1)} %all-gather.3.cloned.1.call-done), kind=kOutput, calls=%fused_computation.48 | convolution fusion | flops 3229614080 | bytes 18956288 | tf_op jit(solution)/shard_map/dot_general | solution.py:76
  217.2 1.4 multiply_convert_fusion
  218.6 0.2 pad_maximum_fusion.2
  218.8 1.8 fusion.21
  220.6 8.2 %collective-permute-start.1 = (bf16[2,1,1,64,5632]{4,3,2,1,0:T(8,128)(2,1)}, bf16[2,1,1,64,5632]{4,3,2,1,0:T(8,128)(2,1)}, u32[]{:S(2)}, u32[]{:S(2)}) collective-permute-start(bf16[2,1,1,64,5632]{4,3,2,1,0:T(8,128)(2,1)} %get-tuple-element.18), channel_id=1, source_target_pairs={{1,0},{2,1},{3,2},{4,3},{5,4},{6,5},{7,6},{8,7},{9,8},{10,9},{11,1... | collective-permute-start | bytes 4325384 | tf_op jit(solution)/shard_map/ppermute | solution.py:22
  228.8 1.9 collective-permute-start
  230.7 1.0 reshape.177
  231.7 5.1 %all-to-all-start = ((bf16[32,2,792]{2,1,0:T(2,128)(2,1)}), bf16[32,2,792]{2,1,0:T(2,128)(2,1)S(1)}, u32[]{:S(2)}, u32[]{:S(2)}) async-start(bf16[32,2,792]{2,1,0:T(2,128)(2,1)} %reshape.177), calls=%async_computation | async-start | bytes 229376 | tf_op jit(solution)/shard_map/all_to_all | solution.py:9
  236.9 17.8 %all-to-all-done = bf16[32,2,792]{2,1,0:T(2,128)(2,1)S(1)} async-done(((bf16[32,2,792]{2,1,0:T(2,128)(2,1)}), bf16[32,2,792]{2,1,0:T(2,128)(2,1)S(1)}, u32[]{:S(2)}, u32[]{:S(2)}) %all-to-all-start) | async-done | bytes 101408 | tf_op jit(solution)/shard_map/all_to_all | solution.py:9
  254.7 0.5 reshape.178
  255.1 0.8 fusion.20
  255.9 0.1 reshape.154
  256.0 0.1 reshape.153
  256.1 0.1 reshape.152
  256.2 0.1 reshape.151
  256.3 0.1 reshape.150
  256.4 0.1 reshape.149
  256.5 0.1 reshape.148
  256.6 0.1 reshape.147
  256.7 0.1 reshape.146
  256.8 3.8 %fusion.5 = bf16[2,1,4,66,5632]{4,3,2,1,0:T(8,128)(2,1)S(1)} fusion(bf16[2,1,1,64,5632]{4,3,2,1,0:T(8,128)(2,1)} %collective-permute-done.1, bf16[2,1,2,64,5632]{4,3,2,1,0:T(8,128)(2,1)S(1)} %bitcast.23, bf16[2,1,1,64,5632]{4,3,2,1,0:T(8,128)(2,1)} %collective-permute-done), kind=kLoop, calls=%fused_computation.7 | loop fusion | flops 35684352 | bytes 11714560 | tf_op jit(solution)/shard_map/concatenate | solution.py:18
  260.6 6.8 %multiply_add_fusion = f32[2,1,2,64,5632]{4,3,2,1,0:T(8,128)S(1)} fusion(bf16[2,1,2,64,5632]{4,3,2,1,0:T(8,128)(2,1)S(1)} %bitcast.24, bf16[2,1,4,66,5632]{4,3,2,1,0:T(8,128)(2,1)S(1)} %fusion.5, bf16[2,1,1,64,5632]{4,3,2,1,0:T(8,128)(2,1)} %collective-permute-done.1, bf16[2,1,1,64,5632]{4,3,2,1,0:T(8,128)(2,1)} %collective-permute-done, ...), kind=kLoop, calls=%fused_computation.8 | loop fusion | flops 40370176 | bytes 29038592 | tf_op jit(solution)/shard_map/add | solution.py:43
  267.4 0.2 slice_bitcast_fusion
  267.6 0.3 fusion.6
  267.9 1.9 fusion.10
  (21 shorter events, 0.2 us)
Async XLA Ops:
  7.2 62.7 %copy-start.3 = (bf16[176]{0:T(256)(128)(2,1)S(1)}, bf16[176]{0:T(256)(128)(2,1)}, u32[]{:S(2)}) copy-start(bf16[176]{0:T(256)(128)(2,1)} %param.9) | copy-start | bytes 1060
  7.2 63.0 %copy-start.4 = (bf16[176]{0:T(256)(128)(2,1)S(1)}, bf16[176]{0:T(256)(128)(2,1)}, u32[]{:S(2)}) copy-start(bf16[176]{0:T(256)(128)(2,1)} %param.11) | copy-start | bytes 1060
  7.2 202.9 %copy-start = (bf16[1,2,64,1120]{3,2,1,0:T(8,128)(2,1)S(1)}, bf16[1,2,64,1120]{3,2,1,0:T(8,128)(2,1)}, u32[]{:S(2)}) copy-start(bf16[1,2,64,1120]{3,2,1,0:T(8,128)(2,1)} %param.7) | copy-start | bytes 860164
  7.2 202.9 %copy-start.1 = (bf16[1,2,64,1120]{3,2,1,0:T(8,128)(2,1)S(1)}, bf16[1,2,64,1120]{3,2,1,0:T(8,128)(2,1)}, u32[]{:S(2)}) copy-start(bf16[1,2,64,1120]{3,2,1,0:T(8,128)(2,1)} %param.6) | copy-start | bytes 860164
  7.2 203.0 %all-gather.3.cloned.1.call-start = ((), (), s32[]{:S(2)}) async-start(), calls=%async_computation.1 | async-start | bytes 13381632 | tf_op jit(solution)/shard_map/all_gather | solution.py:78
  218.8 11.9 %copy-start.2 = (bf16[9,176]{1,0:T(8,128)(2,1)S(1)}, bf16[9,176]{1,0:T(8,128)(2,1)}, u32[]{:S(2)}) copy-start(bf16[9,176]{1,0:T(8,128)(2,1)} %param.10) | copy-start | bytes 9508
  220.6 36.2 %collective-permute-start.1 = (bf16[2,1,1,64,5632]{4,3,2,1,0:T(8,128)(2,1)}, bf16[2,1,1,64,5632]{4,3,2,1,0:T(8,128)(2,1)}, u32[]{:S(2)}, u32[]{:S(2)}) collective-permute-start(bf16[2,1,1,64,5632]{4,3,2,1,0:T(8,128)(2,1)} %get-tuple-element.18), channel_id=1, source_target_pairs={{1,0},{2,1},{3,2},{4,3},{5,4},{6,5},{7,6},{8,7},{9,8},{10,9},{11,1... | collective-permute-start | bytes 4325384 | tf_op jit(solution)/shard_map/ppermute | solution.py:22
  228.8 28.0 %collective-permute-start = (bf16[2,1,1,64,5632]{4,3,2,1,0:T(8,128)(2,1)}, bf16[2,1,1,64,5632]{4,3,2,1,0:T(8,128)(2,1)}, u32[]{:S(2)}, u32[]{:S(2)}) collective-permute-start(bf16[2,1,1,64,5632]{4,3,2,1,0:T(8,128)(2,1)} %get-tuple-element.17), channel_id=1, source_target_pairs={{0,1},{1,2},{2,3},{3,4},{4,5},{5,6},{6,7},{7,8},{8,9},{9,10},{10,1... | collective-permute-start | bytes 4325384 | tf_op jit(solution)/shard_map/ppermute | solution.py:20
  231.7 22.9 %all-to-all-start = ((bf16[32,2,792]{2,1,0:T(2,128)(2,1)}), bf16[32,2,792]{2,1,0:T(2,128)(2,1)S(1)}, u32[]{:S(2)}, u32[]{:S(2)}) async-start(bf16[32,2,792]{2,1,0:T(2,128)(2,1)} %reshape.177), calls=%async_computation | async-start | bytes 229376 | tf_op jit(solution)/shard_map/all_to_all | solution.py:9
Sparse Core Ops, SparseCore 0:
  68.1 89.3 all-gather.2
